TPU v7x, 32 devices: a whole 2x2x4 slice. The times are simulated.
32 devices in a mesh: groups: 2 (over x), month: 16 (over z, y, core).
Axes of the slice: x: 2, y: 2, z: 4, core: 2. Of those that a mesh axis runs over, the one named last changes fastest.
Arguments:
- shocks: float32 [512, 4096], P('month', 'groups'), parts along dimension 1, may hold values from -6 to 6
- long_mean: float32 [512], P('month'), may hold values from 0 to 0.08
- reversion: float32 [4096], P('groups'), parts along dimension 0, may hold values from 0.1 to 1
- volatility: float32 [4096], P('groups'), parts along dimension 0, may hold values from 0.004 to 0.015
- start_rate: float32 [4096], P('groups'), parts along dimension 0, may hold values from 0 to 0.06
- cash_flows: bfloat16 [3, 512, 24576], P(None, 'month', 'groups'), parts along dimension 2, may hold values from -0.5 to 0.5
Outputs:
- present: bfloat16 [3, 24576, 2048], P(None, ('groups', 'month')), parts along dimension 1
There are 2 independent parts, one for each index of `groups`. A program takes and returns all parts, laid end to end along the dimension named above; an argument that names none is the same for every part. Nothing has to cross between parts.
All inputs are finite; a program needn't handle non-finite values.
Results may differ from a plain program's by a relative error of at most 0.0049.
Values may be sent and summed in bfloat16 or wider, within the bound.
A program may use at most 192 MiB of HBM per device.

v0:
```python
import math
import jax
import jax.numpy as jnp
from jax import lax
from jax.sharding import PartitionSpec as P

month_step = 1.0 / 12.0
root_step = math.sqrt(1.0 / 12.0)
risk_price = 0.15
price_scale = risk_price * math.sqrt(12.0)
price_drift = 0.5 * risk_price * risk_price


def prefix(part, axis, combine, identity):
    place = lax.axis_index(axis)
    gathered = jax.tree.map(lambda a: lax.all_gather(a, axis), part)
    state = jax.tree.map(lambda a, e: jnp.zeros_like(a) + jnp.asarray(e, a.dtype), part, identity)

    def one(hop, state):
        return combine(
            state, jax.tree.map(lambda a: lax.dynamic_index_in_dim(a, hop, 0, False), gathered)
        )

    return lax.fori_loop(0, place, one, state)


def compose(earlier, later):
    return (
        later[0] * earlier[0],
        later[0] * earlier[1] + later[1],
        earlier[2] + later[2] * earlier[0],
        earlier[3] + later[3] + later[2] * earlier[1],
    )


def month_maps(shocks, long_mean, reversion, volatility):
    persist = 1.0 - reversion * month_step
    drive = (reversion * month_step)[None, :] * long_mean[:, None] + (volatility * root_step)[
        None, :
    ] * shocks
    factor = jnp.broadcast_to(persist[None, :], drive.shape)
    extra = drive + price_scale * shocks + price_drift
    return lax.associative_scan(compose, (factor, drive, factor, extra), axis=0)


def discount_from(maps, rate_in, total_in):
    total = total_in[None, :] + maps[2] * rate_in[None, :] + maps[3]
    return jnp.exp(-month_step * total).astype(jnp.bfloat16)


def time_discount(shocks, long_mean, reversion, volatility, start_rate):
    maps = month_maps(shocks, long_mean, reversion, volatility)
    block = tuple((member[-1] for member in maps))
    unit_row = jnp.ones_like(start_rate)
    zero_row = jnp.zeros_like(start_rate)
    before = prefix(block, "month", compose, (unit_row, zero_row, zero_row, zero_row))
    rate_in = before[0] * start_rate + before[1]
    total_in = before[2] * start_rate + before[3]
    return discount_from(maps, rate_in, total_in)


def contract(flows, discount):
    blocks = []
    for leg_index in range(flows.shape[0]):
        value = lax.dot_general(
            flows[leg_index], discount, (((0,), (0,)), ((), ())), preferred_element_type=jnp.float32
        )
        blocks.append(value.astype(jnp.bfloat16))
    return jnp.stack(blocks)


def local(shocks, long_mean, reversion, volatility, start_rate, cash_flows):
    own_flows = lax.all_to_all(cash_flows, "month", split_axis=2, concat_axis=1, tiled=True)
    discount = time_discount(shocks, long_mean, reversion, volatility, start_rate)
    every_month = lax.all_gather(discount, "month", axis=0, tiled=True)
    return contract(own_flows, every_month)


def solution(mesh):
    placed = (
        P("month", "groups"),
        P("month"),
        P("groups"),
        P("groups"),
        P("groups"),
        P(None, "month", "groups"),
    )
    return jax.shard_map(
        local,
        mesh=mesh,
        in_specs=placed,
        out_specs=P(None, ("groups", "month"), None),
        check_vma=False,
    )
```

profile of v0, /device:TPU:0, one launch (start us, length us, event | category | flops | bytes accessed | tf_op | source)
XLA Modules:
  0.0 273.4 jit_solution(5829222085009719674)
XLA Ops:
  6.5 15.3 %copy.13 = bf16[3,32,12288]{1,0,2:T(4,128)(2,1)} copy(bf16[3,32,12288]{2,1,0:T(8,128)(2,1)} %param.13) | data formatting | bytes 4718592 | tf_op args[5]
  21.8 15.7 %reshape.39 = bf16[16,2,36864]{2,1,0:T(2,128)(2,1)} reshape(bf16[12288,3,32]{2,1,0:T(4,128)(2,1)} %bitcast.69) | data formatting | bytes 4718592
  37.5 7.6 %all-to-all-start = ((bf16[16,2,36864]{2,1,0:T(2,128)(2,1)}), bf16[16,2,36864]{2,1,0:T(2,128)(2,1)S(1)}, u32[]{:S(2)}, u32[]{:S(2)}) async-start(bf16[16,2,36864]{2,1,0:T(2,128)(2,1)} %reshape.39), calls=%async_computation | async-start | bytes 4718592 | tf_op jit(solution)/shard_map/all_to_all | solution.py:73
  49.9 0.7 multiply_add_fusion.6
  50.6 0.7 pad_maximum_fusion.6
  51.3 0.7 pad_maximum_fusion.8
  53.5 0.7 add_multiply_fusion.1
  54.2 0.9 pad_maximum_fusion.7
  55.1 0.9 pad.153
  56.0 0.9 add_add_fusion.2
  57.1 43.2 %all-gather.2 = f32[16,1,2048]{2,1,0:T(1,128)S(1)} all-gather(f32[1,1,2048]{2,1,0:T(1,128)S(1)} %add_bitcast_fusion.1), channel_id=1, replica_groups=mesh['groups'=2,'month'=16] {'month'}, dimensions={0}, use_global_device_ids=true | all-gather | bytes 139264 | tf_op jit(solution)/shard_map/all_gather | solution.py:16
  100.3 0.7 copy.29
  101.0 0.7 pad_maximum_fusion.4
  101.8 1.0 pad.165
  102.8 28.5 %all-gather.3 = f32[16,1,2048]{2,1,0:T(1,128)S(1)} all-gather(f32[1,1,2048]{2,1,0:T(1,128)S(1)} %add_bitcast_fusion), channel_id=1, replica_groups=mesh['groups'=2,'month'=16] {'month'}, dimensions={0}, use_global_device_ids=true | all-gather | bytes 139264 | tf_op jit(solution)/shard_map/all_gather | solution.py:16
  131.3 0.7 copy.28
  132.0 2.3 pad.299
  134.4 1.4 pad.301
  135.8 0.9 add_bitcast_fusion.2
  136.7 17.8 %all-gather.1 = f32[16,1,2048]{2,1,0:T(1,128)S(1)} all-gather(f32[1,1,2048]{2,1,0:T(1,128)S(1)} %get-tuple-element.132), channel_id=1, replica_groups=mesh['groups'=2,'month'=16] {'month'}, dimensions={0}, use_global_device_ids=true | all-gather | bytes 139264 | tf_op jit(solution)/shard_map/all_gather | solution.py:16
  154.5 0.7 copy.30
  155.2 19.1 %all-gather = f32[16,1,2048]{2,1,0:T(1,128)S(1)} all-gather(f32[1,1,2048]{2,1,0:T(1,128)S(1)} %get-tuple-element.133), channel_id=1, replica_groups=mesh['groups'=2,'month'=16] {'month'}, dimensions={0}, use_global_device_ids=true | all-gather | bytes 139264 | tf_op jit(solution)/shard_map/all_gather | solution.py:16
  174.3 0.7 copy.31
  175.2 0.7 exponential_convert_fusion
  176.0 11.8 %reshape.40 = bf16[12288,3,32]{2,1,0:T(4,128)(2,1)} reshape(bf16[16,2,36864]{2,1,0:T(2,128)(2,1)S(1)} %all-to-all-done) | data formatting | bytes 4718592
  187.7 11.7 %copy.19 = bf16[3,32,16,768]{3,2,1,0:T(8,128)(2,1)S(1)} copy(bf16[3,32,16,768]{1,0,3,2:T(4,128)(2,1)} %bitcast.68) | data formatting | bytes 4718592 | tf_op jit(solution)/shard_map/all_to_all | solution.py:73
  200.3 41.7 %all-gather.6.cloned.1.call-done = bf16[512,2048]{1,0:T(8,128)(2,1)} async-done(((bf16[32,2048]{1,0:T(8,128)(2,1)}), bf16[512,2048]{1,0:T(8,128)(2,1)}) %all-gather.6.cloned.1.call-update) | async-done | bytes 2097168 | tf_op jit(solution)/shard_map/all_gather | solution.py:75
  242.0 3.6 %fusion.1 = bf16[1,768,2048]{1,2,0:T(8,128)(2,1)S(1)} fusion(bf16[512,2048]{1,0:T(8,128)(2,1)} %all-gather.6.cloned.1.call-done, bf16[512,768]{1,0:T(8,128)(2,1)S(1)} %bitcast.77), kind=kOutput, calls=%fused_computation.12 | convolution fusion | flops 1612185600 | bytes 6029312 | tf_op jit(solution)/shard_map/dot_general | solution.py:65
  245.6 1.9 fusion.2
  247.5 1.9 fusion
  249.4 4.6 %pad_maximum_fusion = bf16[3,768,2048]{1,2,0:T(8,128)(2,1)} fusion(bf16[1,768,2048]{1,2,0:T(8,128)(2,1)S(1)} %fusion.2, bf16[1,768,2048]{1,2,0:T(8,128)(2,1)S(1)} %fusion.1, bf16[1,768,2048]{1,2,0:T(8,128)(2,1)S(1)} %fusion), kind=kLoop, calls=%fused_computation.7 | loop fusion | flops 9437184 | bytes 18874368 | tf_op jit(solution)/shard_map/stack | solution.py:69
  253.9 12.6 %copy.18 = bf16[3,768,2048]{2,1,0:T(8,128)(2,1)} copy(bf16[3,768,2048]{1,2,0:T(8,128)(2,1)} %pad_maximum_fusion) | data formatting | bytes 18874368 | tf_op jit(solution)/shard_map/stack | solution.py:69
  (115 shorter events, 7.1 us)
Async XLA Ops:
  37.5 7.6 %copy-start.2 = (f32[2048]{0:T(1024)S(1)}, f32[2048]{0:T(1024)}, u32[]{:S(2)}) copy-start(f32[2048]{0:T(1024)} %param.10) | copy-start | bytes 24580
  37.5 7.6 %copy-start.3 = (f32[2048]{0:T(1024)S(1)}, f32[2048]{0:T(1024)}, u32[]{:S(2)}) copy-start(f32[2048]{0:T(1024)} %param.11) | copy-start | bytes 24580
  37.5 7.7 %copy-start = (f32[32,2048]{1,0:T(8,128)S(1)}, f32[32,2048]{1,0:T(8,128)}, u32[]{:S(2)}) copy-start(f32[32,2048]{1,0:T(8,128)} %param.8) | copy-start | bytes 786436
  37.5 7.7 %copy-start.4 = (f32[32]{0:T(128)S(1)}, f32[32]{0:T(128)}, u32[]{:S(2)}) copy-start(f32[32]{0:T(128)} %param.9) | copy-start | bytes 388
  37.5 138.4 %all-to-all-start = ((bf16[16,2,36864]{2,1,0:T(2,128)(2,1)}), bf16[16,2,36864]{2,1,0:T(2,128)(2,1)S(1)}, u32[]{:S(2)}, u32[]{:S(2)}) async-start(bf16[16,2,36864]{2,1,0:T(2,128)(2,1)} %reshape.39), calls=%async_computation | async-start | bytes 4718592 | tf_op jit(solution)/shard_map/all_to_all | solution.py:73
  45.1 196.9 %all-gather.6.cloned.1.call-start = ((), (), s32[]{:S(2)}) async-start(), calls=%async_computation.1 | async-start | bytes 2228224 | tf_op jit(solution)/shard_map/all_gather | solution.py:75
  56.0 119.2 %copy-start.1 = (f32[2048]{0:T(1024)S(1)}, f32[2048]{0:T(1024)}, u32[]{:S(2)}) copy-start(f32[2048]{0:T(1024)} %param.12) | copy-start | bytes 24580
  242.0 3.6 %copy-start.5 = (bf16[512,2048]{1,0:T(8,128)(2,1)S(1)}, bf16[512,2048]{1,0:T(8,128)(2,1)}, u32[]{:S(2)}) copy-start(bf16[512,2048]{1,0:T(8,128)(2,1)} %all-gather.6.cloned.1.call-done) | copy-start | bytes 6291460
Sparse Core Ops, SparseCore 0:
  176.1 65.8 all-gather.5
where the time goes:
time: 277 us; the launch traced here: 273 us
  blocking collectives  109 us (39%)
  local copies, waits for them, and re-layouts  79.5 us (29%)
  waiting for transfers between devices  41.7 us (15%)
  other arithmetic  14.3 us (5%)
  between operations  14.1 us (5%)
  starting transfers between devices  7.6 us (3%)
  matrix products  7.31 us (3%)
    all_gather x4, blocking collectives, prefix(): gathered = jax.tree.map(lambda a: lax.all_gather(a, axis), part)  109 us
    unnamed x21, local copies, waits for them, and re-layouts  49.3 us
    all_gather x1, waiting for transfers between devices, local(): every_month = lax.all_gather(discount, 'month', axis=0, tiled=True)  41.7 us
    another operation x1, local copies, waits for them, and re-layouts, contract(): return jnp.stack(blocks)  12.6 us
    all_to_all x1, local copies, waits for them, and re-layouts, local(): lax.all_to_all(cash_flows, 'month', split_axis=2, concat_axis=1, tiled=True)  11.7 us
    all_to_all x1, starting transfers between devices, local(): lax.all_to_all(cash_flows, 'month', split_axis=2, concat_axis=1, tiled=True)  7.56 us
    dot_general x3, matrix products, contract(): lax.dot_general(flows[leg_index], discount, (((0,), (0,)), ((), ())), pre...  7.31 us
  transfers between devices with their start and end apart: 2, of which 1 were waited for; matrix products, arithmetic and copies ran while one was open for 17% of the time, Pallas kernels for 0%

commit v1 on v0

--- a/solution.py
+++ b/solution.py
@@ -3,12 +3,27 @@
 import jax.numpy as jnp
 from jax import lax
 from jax.sharding import PartitionSpec as P
+from jax.lax import axis_index, ppermute, psum
 
 month_step = 1.0 / 12.0
 root_step = math.sqrt(1.0 / 12.0)
 risk_price = 0.15
 price_scale = risk_price * math.sqrt(12.0)
 price_drift = 0.5 * risk_price * risk_price
+
+
+def _draft_slices(obj, dim_k, v0):
+    answer, near = (obj.shape[:dim_k], obj.shape[dim_k + 1 :])
+    latest = obj.reshape(*answer, v0, -1, *near)
+    return jnp.moveaxis(latest, dim_k, 0)
+
+
+def finish_the_corner(u_in, ndim_at):
+    u_in = jnp.moveaxis(u_in, 0, ndim_at)
+    carry_in = u_in.shape
+    return u_in.reshape(
+        *carry_in[:ndim_at], carry_in[ndim_at] * carry_in[ndim_at + 1], *carry_in[ndim_at + 2 :]
+    )
 
 
 def prefix(part, axis, combine, identity):
@@ -70,7 +85,20 @@
 
 
 def local(shocks, long_mean, reversion, volatility, start_rate, cash_flows):
-    own_flows = lax.all_to_all(cash_flows, "month", split_axis=2, concat_axis=1, tiled=True)
+    k_now = psum(1, axis_name="month")
+    arr_next = axis_index("month")
+    x_new, even = (k_now, arr_next)
+    mat_out = _draft_slices(cash_flows, 2, x_new)
+    row_list = [mat_out[even]]
+    at = 1
+    while at < x_new:
+        inter = mat_out[even ^ at]
+        spare = ppermute(inter, axis_name="month", perm=[(j0, j0 ^ at) for j0 in range(x_new)])
+        row_list.append(spare)
+        at += 1
+    work_now = jnp.stack(row_list, axis=0)
+    mat_out = work_now[even ^ jnp.arange(x_new)]
+    own_flows = finish_the_corner(mat_out, 1)
     discount = time_discount(shocks, long_mean, reversion, volatility, start_rate)
     every_month = lax.all_gather(discount, "month", axis=0, tiled=True)
     return contract(own_flows, every_month)

time: 277 us -> 195 us (0.70)
  the two profiles are of different devices: /device:TPU:0 before, /device:TPU:11 now
where the time goes in v1:
time: 195 us
  blocking collectives  74.4 us (38%)
  waiting for transfers between devices  36.2 us (19%)
  starting transfers between devices  28.1 us (14%)
  local copies, waits for them, and re-layouts  25.8 us (13%)
  between operations  14.5 us (7%)
  other arithmetic  7.72 us (4%)
  matrix products  7.49 us (4%)
    all_gather x4, blocking collectives, prefix(): gathered = jax.tree.map(lambda a: lax.all_gather(a, axis), part)  74.4 us
    ppermute x15, waiting for transfers between devices, local(): ppermute(inter, axis_name='month', perm=[(j0, j0 ^ at) for j0 in range(x_...  36.2 us
    ppermute x15, starting transfers between devices, local(): ppermute(inter, axis_name='month', perm=[(j0, j0 ^ at) for j0 in range(x_...  28.1 us
    unnamed x43, local copies, waits for them, and re-layouts  12.8 us
    dot_general x3, matrix products, contract(): lax.dot_general(flows[leg_index], discount, (((0,), (0,)), ((), ())), pre...  7.49 us
    another operation x2, local copies, waits for them, and re-layouts  6.94 us
    another operation x1, other arithmetic, contract(): return jnp.stack(blocks)  4.12 us
  transfers between devices with their start and end apart: 16, of which 8 were waited for; matrix products, arithmetic and copies ran while one was open for 12% of the time, Pallas kernels for 0%

profile of v1, /device:TPU:11, one launch (start us, length us, event | category | flops | bytes accessed | tf_op | source)
XLA Modules:
  0.0 194.6 jit_solution(13780195377608200824)
XLA Ops:
  7.3 1.1 multiply_add_fusion.3
  11.3 19.7 %all-gather.2 = f32[16,1,2048]{2,1,0:T(1,128)S(1)} all-gather(f32[1,1,2048]{2,1,0:T(1,128)S(1)} %add_bitcast_fusion.1), channel_id=1, replica_groups=mesh['groups'=2,'month'=16] {'month'}, dimensions={0}, use_global_device_ids=true | all-gather | bytes 139264 | tf_op jit(solution)/shard_map/all_gather | solution.py:31
  31.2 17.8 %all-gather.3 = f32[16,1,2048]{2,1,0:T(1,128)S(1)} all-gather(f32[1,1,2048]{2,1,0:T(1,128)S(1)} %add_bitcast_fusion), channel_id=1, replica_groups=mesh['groups'=2,'month'=16] {'month'}, dimensions={0}, use_global_device_ids=true | all-gather | bytes 139264 | tf_op jit(solution)/shard_map/all_gather | solution.py:31
  49.1 19.1 %all-gather.1 = f32[16,1,2048]{2,1,0:T(1,128)S(1)} all-gather(f32[1,1,2048]{2,1,0:T(1,128)S(1)} %get-tuple-element.148), channel_id=1, replica_groups=mesh['groups'=2,'month'=16] {'month'}, dimensions={0}, use_global_device_ids=true | all-gather | bytes 139264 | tf_op jit(solution)/shard_map/all_gather | solution.py:31
  68.3 17.8 %all-gather = f32[16,1,2048]{2,1,0:T(1,128)S(1)} all-gather(f32[1,1,2048]{2,1,0:T(1,128)S(1)} %get-tuple-element.149), channel_id=1, replica_groups=mesh['groups'=2,'month'=16] {'month'}, dimensions={0}, use_global_device_ids=true | all-gather | bytes 139264 | tf_op jit(solution)/shard_map/all_gather | solution.py:31
  87.7 2.2 %copy.27 = bf16[12,8,16,768]{3,2,1,0:T(8,128)(2,1)S(1)} copy(bf16[12,8,16,768]{3,1,2,0:T(8,128)(2,1)} %bitcast.144) | data formatting | bytes 4718592
  90.0 6.9 %constant_dynamic-slice_fusion.4 = (bf16[3,32,1,768]{3,2,1,0:T(2,128)(2,1)S(1)}, bf16[3,32,1,768]{3,2,1,0:T(2,128)(2,1)S(1)}, bf16[3,32,1,768]{3,2,1,0:T(2,128)(...) fusion(bf16[3,32,16,768]{3,2,1,0:T(8,128)(2,1)S(1)} %bitcast.14, ...), kind=kLoop, calls=%fused_computation.134 | loop fusion | bytes 4718656 | tf_op jit(solution)/shard_map/dynamic-slice.15
  97.1 1.7 collective-permute-start.1
  99.4 2.7 %collective-permute-start.3 = (bf16[3,32,768]{2,1,0:T(8,128)(2,1)S(1)}, bf16[3,32,768]{2,1,0:T(8,128)(2,1)S(1)}, u32[]{:S(2)}, u32[]{:S(2)}) collective-permute-start(bf16[3,32,768]{2,1,0:T(8,128)(2,1)S(1)} %bitcast.172), channel_id=1, source_target_pairs={{0,4},{1,5},{2,6},{3,7},{4,0},{5,1},{6,2},{7,3},{8,12},{9,13},{10,... | collective-permute-start | bytes 442376 | tf_op jit(solution)/shard_map/ppermute | solution.py:96
  103.2 2.6 %collective-permute-start.5 = (bf16[3,32,768]{2,1,0:T(8,128)(2,1)S(1)}, bf16[3,32,768]{2,1,0:T(8,128)(2,1)S(1)}, u32[]{:S(2)}, u32[]{:S(2)}) collective-permute-start(bf16[3,32,768]{2,1,0:T(8,128)(2,1)S(1)} %bitcast.175), channel_id=1, source_target_pairs={{0,6},{1,7},{2,4},{3,5},{4,2},{5,3},{6,0},{7,1},{8,14},{9,15},{10,... | collective-permute-start | bytes 442376 | tf_op jit(solution)/shard_map/ppermute | solution.py:96
  106.5 1.6 collective-permute-start.6
  108.8 1.3 collective-permute-start.7
  111.8 6.4 %collective-permute-done.4 = bf16[3,32,768]{2,1,0:T(8,128)(2,1)S(1)} collective-permute-done((bf16[3,32,768]{2,1,0:T(8,128)(2,1)S(1)}, bf16[3,32,768]{2,1,0:T(8,128)(2,1)S(1)}, u32[]{:S(2)}, u32[]{:S(2)}) %collective-permute-start.4) | collective-permute-done | bytes 147488 | tf_op jit(solution)/shard_map/ppermute | solution.py:96
  118.3 5.4 %collective-permute-start.9 = (bf16[3,32,768]{2,1,0:T(8,128)(2,1)S(1)}, bf16[3,32,768]{2,1,0:T(8,128)(2,1)S(1)}, u32[]{:S(2)}, u32[]{:S(2)}) collective-permute-start(bf16[3,32,768]{2,1,0:T(8,128)(2,1)S(1)} %bitcast.167), channel_id=1, source_target_pairs={{0,10},{1,11},{2,8},{3,9},{4,14},{5,15},{6,12},{7,13},{8,2},{9,3},... | collective-permute-start | bytes 442376 | tf_op jit(solution)/shard_map/ppermute | solution.py:96
  124.4 1.1 collective-permute-done.5
  125.5 5.5 %collective-permute-start.10 = (bf16[3,32,768]{2,1,0:T(8,128)(2,1)S(1)}, bf16[3,32,768]{2,1,0:T(8,128)(2,1)S(1)}, u32[]{:S(2)}, u32[]{:S(2)}) collective-permute-start(bf16[3,32,768]{2,1,0:T(8,128)(2,1)S(1)} %bitcast.166), channel_id=1, source_target_pairs={{0,11},{1,10},{2,9},{3,8},{4,15},{5,14},{6,13},{7,12},{8,3},{9,2},... | collective-permute-start | bytes 442376 | tf_op jit(solution)/shard_map/ppermute | solution.py:96
  131.7 1.2 collective-permute-start.11
  133.6 1.7 collective-permute-start.12
  135.9 1.5 collective-permute-start.13
  138.1 12.6 %collective-permute-done.9 = bf16[3,32,768]{2,1,0:T(8,128)(2,1)S(1)} collective-permute-done((bf16[3,32,768]{2,1,0:T(8,128)(2,1)S(1)}, bf16[3,32,768]{2,1,0:T(8,128)(2,1)S(1)}, u32[]{:S(2)}, u32[]{:S(2)}) %collective-permute-start.9) | collective-permute-done | bytes 147488 | tf_op jit(solution)/shard_map/ppermute | solution.py:96
  150.7 1.6 collective-permute-start.14
  153.0 0.9 collective-permute-done.10
  154.5 6.8 %collective-permute-done.11 = bf16[3,32,768]{2,1,0:T(8,128)(2,1)S(1)} collective-permute-done((bf16[3,32,768]{2,1,0:T(8,128)(2,1)S(1)}, bf16[3,32,768]{2,1,0:T(8,128)(2,1)S(1)}, u32[]{:S(2)}, u32[]{:S(2)}) %collective-permute-start.11) | collective-permute-done | bytes 147488 | tf_op jit(solution)/shard_map/ppermute | solution.py:96
  162.0 2.5 %collective-permute-done.12 = bf16[3,32,768]{2,1,0:T(8,128)(2,1)S(1)} collective-permute-done((bf16[3,32,768]{2,1,0:T(8,128)(2,1)S(1)}, bf16[3,32,768]{2,1,0:T(8,128)(2,1)S(1)}, u32[]{:S(2)}, u32[]{:S(2)}) %collective-permute-start.12) | collective-permute-done | bytes 147488 | tf_op jit(solution)/shard_map/ppermute | solution.py:96
  165.1 3.4 %collective-permute-done.13 = bf16[3,32,768]{2,1,0:T(8,128)(2,1)S(1)} collective-permute-done((bf16[3,32,768]{2,1,0:T(8,128)(2,1)S(1)}, bf16[3,32,768]{2,1,0:T(8,128)(2,1)S(1)}, u32[]{:S(2)}, u32[]{:S(2)}) %collective-permute-start.13) | collective-permute-done | bytes 147488 | tf_op jit(solution)/shard_map/ppermute | solution.py:96
  169.2 2.5 %collective-permute-done.14 = bf16[3,32,768]{2,1,0:T(8,128)(2,1)S(1)} collective-permute-done((bf16[3,32,768]{2,1,0:T(8,128)(2,1)S(1)}, bf16[3,32,768]{2,1,0:T(8,128)(2,1)S(1)}, u32[]{:S(2)}, u32[]{:S(2)}) %collective-permute-start.14) | collective-permute-done | bytes 147488 | tf_op jit(solution)/shard_map/ppermute | solution.py:96
  172.4 2.4 %gather_fusion = bf16[16,3,32,768]{3,2,1,0:T(8,128)(2,1)S(1)} fusion(bf16[16,3,32,768]{3,2,1,0:T(8,128)(2,1)} %bitcast_dynamic-update-slice_fusion.1, s32[1024]{0:T(1024)S(1)} %pad_clamp_fusion), kind=kCustom, calls=%fused_computation | custom fusion | bytes 4718656 | tf_op jit(solution)/shard_map/gather | solution.py:100
  174.8 1.3 fusion.19
  176.1 3.8 %fusion.2 = bf16[1,768,2048]{2,1,0:T(8,128)(2,1)S(1)} fusion(bf16[512,768]{1,0:T(8,128)(2,1)} %bitcast.151, bf16[512,2048]{1,0:T(8,128)(2,1)} %all-gather.6.cloned.1.call-done), kind=kOutput, calls=%fused_computation.14 | convolution fusion | flops 1612185600 | bytes 6029312 | tf_op jit(solution)/shard_map/dot_general | solution.py:80
  179.9 1.8 fusion
  181.8 1.8 fusion.1
  183.6 4.1 %pad_maximum_fusion = bf16[3,768,2048]{2,1,0:T(8,128)(2,1)} fusion(bf16[1,768,2048]{2,1,0:T(8,128)(2,1)S(1)} %fusion.2, bf16[1,768,2048]{2,1,0:T(8,128)(2,1)S(1)} %fusion.1, bf16[1,768,2048]{2,1,0:T(8,128)(2,1)S(1)} %fusion), kind=kLoop, calls=%fused_computation.8 | loop fusion | flops 9437184 | bytes 18874368 | tf_op jit(solution)/shard_map/stack | solution.py:84
  (180 shorter events, 17.5 us)
Async XLA Ops:
  6.5 169.5 %all-gather.6.cloned.1.call-start = ((), (), s32[]{:S(2)}) async-start(), calls=%async_computation | async-start | bytes 2228224 | tf_op jit(solution)/shard_map/all_gather | solution.py:103
  11.3 75.6 %copy-start.1 = (f32[2048]{0:T(1024)S(1)}, f32[2048]{0:T(1024)}, u32[]{:S(2)}) copy-start(f32[2048]{0:T(1024)} %param.12) | copy-start | bytes 24580
  97.0 6.3 %collective-permute-start = (bf16[3,32,768]{2,1,0:T(8,128)(2,1)S(1)}, bf16[3,32,768]{2,1,0:T(8,128)(2,1)S(1)}, u32[]{:S(2)}, u32[]{:S(2)}) collective-permute-start(bf16[3,32,768]{2,1,0:T(8,128)(2,1)S(1)} %bitcast.176), channel_id=1, source_target_pairs={{0,1},{1,0},{2,3},{3,2},{4,5},{5,4},{6,7},{7,6},{8,9},{9,8},{10,11... | collective-permute-start | bytes 442376 | tf_op jit(solution)/shard_map/ppermute | solution.py:96
  97.1 9.4 %collective-permute-start.1 = (bf16[3,32,768]{2,1,0:T(8,128)(2,1)S(1)}, bf16[3,32,768]{2,1,0:T(8,128)(2,1)S(1)}, u32[]{:S(2)}, u32[]{:S(2)}) collective-permute-start(bf16[3,32,768]{2,1,0:T(8,128)(2,1)S(1)} %bitcast.174), channel_id=1, source_target_pairs={{0,2},{1,3},{2,0},{3,1},{4,6},{5,7},{6,4},{7,5},{8,10},{9,11},{10,... | collective-permute-start | bytes 442376 | tf_op jit(solution)/shard_map/ppermute | solution.py:96
  98.8 10.0 %collective-permute-start.2 = (bf16[3,32,768]{2,1,0:T(8,128)(2,1)S(1)}, bf16[3,32,768]{2,1,0:T(8,128)(2,1)S(1)}, u32[]{:S(2)}, u32[]{:S(2)}) collective-permute-start(bf16[3,32,768]{2,1,0:T(8,128)(2,1)S(1)} %bitcast.173), channel_id=1, source_target_pairs={{0,3},{1,2},{2,1},{3,0},{4,7},{5,6},{6,5},{7,4},{8,11},{9,10},{10,... | collective-permute-start | bytes 442376 | tf_op jit(solution)/shard_map/ppermute | solution.py:96
  99.4 11.4 %collective-permute-start.3 = (bf16[3,32,768]{2,1,0:T(8,128)(2,1)S(1)}, bf16[3,32,768]{2,1,0:T(8,128)(2,1)S(1)}, u32[]{:S(2)}, u32[]{:S(2)}) collective-permute-start(bf16[3,32,768]{2,1,0:T(8,128)(2,1)S(1)} %bitcast.172), channel_id=1, source_target_pairs={{0,4},{1,5},{2,6},{3,7},{4,0},{5,1},{6,2},{7,3},{8,12},{9,13},{10,... | collective-permute-start | bytes 442376 | tf_op jit(solution)/shard_map/ppermute | solution.py:96
  102.0 16.2 %collective-permute-start.4 = (bf16[3,32,768]{2,1,0:T(8,128)(2,1)S(1)}, bf16[3,32,768]{2,1,0:T(8,128)(2,1)S(1)}, u32[]{:S(2)}, u32[]{:S(2)}) collective-permute-start(bf16[3,32,768]{2,1,0:T(8,128)(2,1)S(1)} %bitcast.170), channel_id=1, source_target_pairs={{0,5},{1,4},{2,7},{3,6},{4,1},{5,0},{6,3},{7,2},{8,13},{9,12},{10,... | collective-permute-start | bytes 442376 | tf_op jit(solution)/shard_map/ppermute | solution.py:96
  103.2 22.3 %collective-permute-start.5 = (bf16[3,32,768]{2,1,0:T(8,128)(2,1)S(1)}, bf16[3,32,768]{2,1,0:T(8,128)(2,1)S(1)}, u32[]{:S(2)}, u32[]{:S(2)}) collective-permute-start(bf16[3,32,768]{2,1,0:T(8,128)(2,1)S(1)} %bitcast.175), channel_id=1, source_target_pairs={{0,6},{1,7},{2,4},{3,5},{4,2},{5,3},{6,0},{7,1},{8,14},{9,15},{10,... | collective-permute-start | bytes 442376 | tf_op jit(solution)/shard_map/ppermute | solution.py:96
  106.5 25.1 %collective-permute-start.6 = (bf16[3,32,768]{2,1,0:T(8,128)(2,1)S(1)}, bf16[3,32,768]{2,1,0:T(8,128)(2,1)S(1)}, u32[]{:S(2)}, u32[]{:S(2)}) collective-permute-start(bf16[3,32,768]{2,1,0:T(8,128)(2,1)S(1)} %bitcast.171), channel_id=1, source_target_pairs={{0,7},{1,6},{2,5},{3,4},{4,3},{5,2},{6,1},{7,0},{8,15},{9,14},{10,... | collective-permute-start | bytes 442376 | tf_op jit(solution)/shard_map/ppermute | solution.py:96
  108.8 24.8 %collective-permute-start.7 = (bf16[3,32,768]{2,1,0:T(8,128)(2,1)S(1)}, bf16[3,32,768]{2,1,0:T(8,128)(2,1)S(1)}, u32[]{:S(2)}, u32[]{:S(2)}) collective-permute-start(bf16[3,32,768]{2,1,0:T(8,128)(2,1)S(1)} %bitcast.169), channel_id=1, source_target_pairs={{0,8},{1,9},{2,10},{3,11},{4,12},{5,13},{6,14},{7,15},{8,0},{9,1},... | collective-permute-start | bytes 442376 | tf_op jit(solution)/shard_map/ppermute | solution.py:96
  110.8 25.1 %collective-permute-start.8 = (bf16[3,32,768]{2,1,0:T(8,128)(2,1)S(1)}, bf16[3,32,768]{2,1,0:T(8,128)(2,1)S(1)}, u32[]{:S(2)}, u32[]{:S(2)}) collective-permute-start(bf16[3,32,768]{2,1,0:T(8,128)(2,1)S(1)} %bitcast.168), channel_id=1, source_target_pairs={{0,9},{1,8},{2,11},{3,10},{4,13},{5,12},{6,15},{7,14},{8,1},{9,0},... | collective-permute-start | bytes 442376 | tf_op jit(solution)/shard_map/ppermute | solution.py:96
  118.3 32.4 %collective-permute-start.9 = (bf16[3,32,768]{2,1,0:T(8,128)(2,1)S(1)}, bf16[3,32,768]{2,1,0:T(8,128)(2,1)S(1)}, u32[]{:S(2)}, u32[]{:S(2)}) collective-permute-start(bf16[3,32,768]{2,1,0:T(8,128)(2,1)S(1)} %bitcast.167), channel_id=1, source_target_pairs={{0,10},{1,11},{2,8},{3,9},{4,14},{5,15},{6,12},{7,13},{8,2},{9,3},... | collective-permute-start | bytes 442376 | tf_op jit(solution)/shard_map/ppermute | solution.py:96
  125.5 28.4 %collective-permute-start.10 = (bf16[3,32,768]{2,1,0:T(8,128)(2,1)S(1)}, bf16[3,32,768]{2,1,0:T(8,128)(2,1)S(1)}, u32[]{:S(2)}, u32[]{:S(2)}) collective-permute-start(bf16[3,32,768]{2,1,0:T(8,128)(2,1)S(1)} %bitcast.166), channel_id=1, source_target_pairs={{0,11},{1,10},{2,9},{3,8},{4,15},{5,14},{6,13},{7,12},{8,3},{9,2},... | collective-permute-start | bytes 442376 | tf_op jit(solution)/shard_map/ppermute | solution.py:96
  131.7 29.6 %collective-permute-start.11 = (bf16[3,32,768]{2,1,0:T(8,128)(2,1)S(1)}, bf16[3,32,768]{2,1,0:T(8,128)(2,1)S(1)}, u32[]{:S(2)}, u32[]{:S(2)}) collective-permute-start(bf16[3,32,768]{2,1,0:T(8,128)(2,1)S(1)} %bitcast.165), channel_id=1, source_target_pairs={{0,12},{1,13},{2,14},{3,15},{4,8},{5,9},{6,10},{7,11},{8,4},{9,5},... | collective-permute-start | bytes 442376 | tf_op jit(solution)/shard_map/ppermute | solution.py:96
  133.6 30.9 %collective-permute-start.12 = (bf16[3,32,768]{2,1,0:T(8,128)(2,1)S(1)}, bf16[3,32,768]{2,1,0:T(8,128)(2,1)S(1)}, u32[]{:S(2)}, u32[]{:S(2)}) collective-permute-start(bf16[3,32,768]{2,1,0:T(8,128)(2,1)S(1)} %bitcast.164), channel_id=1, source_target_pairs={{0,13},{1,12},{2,15},{3,14},{4,9},{5,8},{6,11},{7,10},{8,5},{9,4},... | collective-permute-start | bytes 442376 | tf_op jit(solution)/shard_map/ppermute | solution.py:96
  135.9 32.6 %collective-permute-start.13 = (bf16[3,32,768]{2,1,0:T(8,128)(2,1)S(1)}, bf16[3,32,768]{2,1,0:T(8,128)(2,1)S(1)}, u32[]{:S(2)}, u32[]{:S(2)}) collective-permute-start(bf16[3,32,768]{2,1,0:T(8,128)(2,1)S(1)} %bitcast.163), channel_id=1, source_target_pairs={{0,14},{1,15},{2,12},{3,13},{4,10},{5,11},{6,8},{7,9},{8,6},{9,7},... | collective-permute-start | bytes 442376 | tf_op jit(solution)/shard_map/ppermute | solution.py:96
  150.7 21.0 %collective-permute-start.14 = (bf16[3,32,768]{2,1,0:T(8,128)(2,1)S(1)}, bf16[3,32,768]{2,1,0:T(8,128)(2,1)S(1)}, u32[]{:S(2)}, u32[]{:S(2)}) collective-permute-start(bf16[3,32,768]{2,1,0:T(8,128)(2,1)S(1)} %bitcast.162), channel_id=1, source_target_pairs={{0,15},{1,14},{2,13},{3,12},{4,11},{5,10},{6,9},{7,8},{8,7},{9,6},... | collective-permute-start | bytes 442376 | tf_op jit(solution)/shard_map/ppermute | solution.py:96
  176.1 3.8 %copy-start = (bf16[1,16,32,768]{3,2,0,1:T(8,128)(2,1)S(1)}, bf16[1,16,32,768]{3,2,0,1:T(8,128)(2,1)}, u32[]{:S(2)}) copy-start(bf16[1,16,32,768]{3,2,0,1:T(8,128)(2,1)} %get-tuple-element.93) | copy-start | bytes 2359300
  176.1 3.8 %copy-start.2 = (bf16[512,2048]{1,0:T(8,128)(2,1)S(1)}, bf16[512,2048]{1,0:T(8,128)(2,1)}, u32[]{:S(2)}) copy-start(bf16[512,2048]{1,0:T(8,128)(2,1)} %all-gather.6.cloned.1.call-done) | copy-start | bytes 6291460
Sparse Core Ops, SparseCore 0:
  87.8 61.7 all-gather.5
